TPU v7x, 32 devices: a whole 2x2x4 slice. The times are simulated.
32 devices in a mesh: section: 4 (over z), dp: 8 (over y, x, core).
Axes of the slice: x: 2, y: 2, z: 4, core: 2. Of those that a mesh axis runs over, the one named last changes fastest.
Arguments:
- gradient: float32 [4, 8, 256, 4096], P('section', 'dp'), may hold values from -6 to 6
- dither: int32 [4, 8, 256, 4096], P('section', 'dp'), may hold values from 0 to 255
- sign_bits: int32 [4096], replicated, may hold values from 0 to 1
- levels: float32 [16], replicated, may hold values from -1 to 1, as said below
- layout: int32 [256], replicated, may hold values from 0 to 255, each once
- master: float32 [4, 256, 4096], P('section', 'dp'), may hold values from -6 to 6
- first_moment: float32 [4, 256, 4096], P('section', 'dp'), may hold values from -4 to 4
- second_moment: float32 [4, 256, 4096], P('section', 'dp'), may hold values from 0.05 to 2
Outputs:
- updated_master: float32 [4, 256, 4096], P('section', 'dp')
- updated_first: float32 [4, 256, 4096], P('section', 'dp')
- updated_second: float32 [4, 256, 4096], P('section', 'dp')
- parameters: bfloat16 [4, 256, 4096], P('section')
Inputs may be any that keep to these rules, and one draw needn't show every extreme that they name: `levels`: strictly increasing; the first is -1 and the last 1; neighbouring levels differ by at least 1/30. `layout`: each block number once.
All inputs are finite; a program needn't handle non-finite values.
Results may differ from a plain program's by a relative error of at most 0.001.
The roundings to bfloat16 on the way count: a program that leaves them out, or rounds other values in their place, can miss the bound.
Values may be sent and summed in bfloat16 or wider, within the bound.
A program may use at most 64 MiB of HBM per device.

v0:
```python
import math

import jax
import jax.numpy as jnp
from jax import lax
from jax.sharding import PartitionSpec as P

adam_epsilon = 1e-08
learning_rate = 0.02
weight_decay = 0.1
first_decay = 0.9
second_decay = 0.95
dither_steps = 256.0


def hadamard_table(edge_length):
    row_numbers = lax.broadcasted_iota(jnp.int32, (edge_length, edge_length), 0)
    column_numbers = lax.broadcasted_iota(jnp.int32, (edge_length, edge_length), 1)
    common = jnp.bitwise_and(row_numbers, column_numbers)
    parity = jnp.zeros((edge_length, edge_length), jnp.int32)
    for bit_number in range(edge_length.bit_length() - 1):
        parity = parity + jnp.bitwise_and(jnp.right_shift(common, bit_number), 1)
    parity = parity % 2
    return (1 - 2 * parity).astype(jnp.float32)


def square_transform(blocks):
    edge_length = math.isqrt(blocks.shape[-1])
    table = hadamard_table(edge_length)
    folded = blocks.reshape(-1, edge_length, edge_length)
    turned = jnp.einsum("ac,ncd,db->nab", table, folded, table, precision=lax.Precision.HIGHEST)
    return turned.reshape(blocks.shape) / edge_length


def rotate(blocks, flips):
    return square_transform(blocks * flips)


def unrotate(blocks, flips):
    return square_transform(blocks) * flips


def encode(ratios, levels):
    relaxed = jnp.zeros_like(ratios)
    for position in range(levels.shape[0] - 1):
        spacing = levels[position + 1] - levels[position]
        relaxed = relaxed + jnp.clip((ratios - levels[position]) / spacing, 0.0, 1.0)
    return relaxed


def decode(symbols, levels):
    values = jnp.zeros_like(symbols) + levels[0]
    for position in range(levels.shape[0] - 1):
        spacing = levels[position + 1] - levels[position]
        values = values + spacing * jnp.clip(symbols - position, 0.0, 1.0)
    return values


def local(gradient, dither, sign_bits, levels, layout, master, first_moment, second_moment):
    flips = (1 - 2 * sign_bits).astype(jnp.float32)
    rotated = rotate(gradient[0, 0], flips)
    peaks = jnp.max(jnp.abs(rotated), axis=1)
    block_scale = lax.pmax(peaks, "dp") + 1e-06
    offsets = (dither[0, 0].astype(jnp.float32) + 0.5) / dither_steps - 0.5
    symbols = (encode(rotated / block_scale[:, None], levels) + offsets).astype(jnp.bfloat16)
    slotted = jnp.take(symbols, layout, axis=0)
    groups = lax.axis_size("dp")
    block_count = slotted.shape[0]
    owned = block_count // groups
    first_slot = lax.axis_index("dp") * owned
    slot_scale = lax.dynamic_slice_in_dim(jnp.take(block_scale, layout), first_slot, owned)
    summed_codes = jnp.sum(
        decode(
            lax.all_to_all(
                slotted.reshape(groups, owned, slotted.shape[1]),
                "dp",
                split_axis=0,
                concat_axis=0,
                tiled=True,
            ).astype(jnp.float32),
            levels,
        ),
        axis=0,
    )
    grads = unrotate(summed_codes * slot_scale[:, None], flips)
    updated_first = first_decay * first_moment[0] + (1.0 - first_decay) * grads
    updated_second = second_decay * second_moment[0] + (1.0 - second_decay) * grads * grads
    updated_master = master[0] - learning_rate * (
        updated_first / (jnp.sqrt(updated_second) + adam_epsilon) + weight_decay * master[0]
    )
    gathered = lax.all_gather(updated_master.astype(jnp.bfloat16), "dp", axis=0, tiled=True)
    inverse = jnp.argsort(layout)
    parameters = jnp.take(gathered, inverse, axis=0)
    return (updated_master[None], updated_first[None], updated_second[None], parameters[None])


def solution(mesh):
    placed = (
        P("section", "dp", None, None),
        P("section", "dp", None, None),
        P(),
        P(),
        P(),
        P("section", "dp", None),
        P("section", "dp", None),
        P("section", "dp", None),
    )
    return jax.shard_map(
        local,
        mesh=mesh,
        in_specs=placed,
        out_specs=(
            P("section", "dp", None),
            P("section", "dp", None),
            P("section", "dp", None),
            P("section", None, None),
        ),
        check_vma=False,
    )
```

profile of v0, /device:TPU:0, one launch (start us, length us, event | category | flops | bytes accessed | tf_op | source)
XLA Modules:
  0.0 184.5 jit_solution(1243858689755332125)
XLA Ops:
  7.2 5.6 %copy.14 = f32[1,1,256,4096]{2,3,1,0:T(8,128)} copy(f32[1,1,256,4096]{3,2,1,0:T(8,128)} %param.10) | data formatting | bytes 8388608 | tf_op args[0]
  12.8 0.1 mul.245
  12.9 2.6 %broadcast_multiply_fusion = f32[256,64,64]{0,2,1:T(8,128)S(1)} fusion(f32[256,64,64]{0,2,1:T(8,128)} %bitcast.52, f32[64,64]{1,0:T(8,128)S(1)} %mul.245), kind=kLoop, calls=%fused_computation.72 | loop fusion | flops 1048576 | bytes 8404992 | tf_op jit(solution)/shard_map/mul | solution.py:36
  15.4 6.6 %fusion.47 = f32[256,64,64]{0,2,1:T(8,128)S(1)} fusion(f32[256,64,64]{0,2,1:T(8,128)S(1)} %broadcast_multiply_fusion), kind=kOutput, calls=%fused_computation.66 | convolution fusion | flops 805437440 | bytes 8388608 | tf_op jit(solution)/shard_map/ac,ncd,db->nab/dot_general | solution.py:31
  22.1 7.0 %abs_reduce_fusion = (f32[256]{0:T(256)S(1)}, f32[256,64,64]{0,2,1:T(8,128)}) fusion(f32[256,64,64]{0,2,1:T(8,128)S(1)} %fusion.47), kind=kOutput, calls=%fused_computation.68 | convolution fusion | flops 808582912 | bytes 8389632 | tf_op jit(solution)/shard_map/ac,ncd,db->nab/dot_general | solution.py:31
  29.1 5.6 %copy.16 = f32[256,4096]{1,0:T(8,128)} copy(f32[256,4096]{0,1:T(8,128)} %bitcast.53) | data formatting | bytes 8388608 | tf_op jit(solution)/shard_map/div | solution.py:32
  34.8 0.7 fusion.124
  54.1 15.3 %pmax.7 = f32[256]{0:T(256)S(1)} all-reduce(f32[256]{0:T(256)S(1)} %get-tuple-element.28), channel_id=1, replica_groups=mesh['section'=4,'dp'=8] {'dp'}, use_global_device_ids=true, to_apply=%region_1.2 | all-reduce | flops 256 | bytes 2048 | tf_op jit(solution)/shard_map/pmax | solution.py:63
  69.5 1.9 %gather_fusion = f32[256]{0:T(256)S(1)} fusion(f32[256]{0:T(256)S(1)} %broadcast_add_fusion, s32[1024]{0:T(1024)S(1)} %pad_clamp_fusion.1), kind=kCustom, calls=%fused_computation.2 | custom fusion | bytes 3072 | tf_op jit(solution)/shard_map/jit(_take)/gather | solution.py:71
  71.4 20.1 %fusion.44 = bf16[256,4096]{1,0:T(8,128)(2,1)S(1)} fusion(s32[1,1,256,4096]{3,2,1,0:T(8,128)} %param.11, f32[256,4096]{1,0:T(8,128)} %copy.16, f32[]{:T(128)S(6)} %sub.280, f32[]{:T(128)} %bitcast.18, f32[]{:T(128)S(6)} %sub.277, f32[]{:T(128)} %bitcast.17, f32[]{:T(128)S(6)} %sub.274, f32[]{:T(128)} %bitcast.16, f32[]{:T(128)S(6)} %sub.271, f32[]{:T(128)} %bitcast.15, ...), kind=kLoop, calls=%fused_computation.63 | loop fusion | flops 69206016 | bytes 10486904 | tf_op jit(solution)/shard_map/convert_element_type | solution.py:65
  91.5 3.2 %gather_fusion.1 = bf16[256,4096]{1,0:T(8,128)(2,1)} fusion(bf16[256,4096]{1,0:T(8,128)(2,1)S(1)} %fusion.44, s32[1024]{0:T(1024)S(1)} %pad_clamp_fusion.1), kind=kCustom, calls=%fused_computation.clone | custom fusion | bytes 4195328 | tf_op jit(solution)/shard_map/jit(_take)/gather | solution.py:66
  94.7 3.2 %broadcast_select_fusion = bf16[256,4096]{1,0:T(8,128)(2,1)} fusion(bf16[256,4096]{1,0:T(8,128)(2,1)} %gather_fusion.1, pred[256]{0:T(512)(128)(4,1)S(1)} %get-tuple-element.11), kind=kLoop, calls=%fused_computation.73 | loop fusion | flops 1048576 | bytes 4194560 | tf_op jit(solution)/shard_map/jit(_take)/select_n | solution.py:66
  97.9 3.6 %all-to-all-start = ((bf16[8,32,4096]{2,1,0:T(8,128)(2,1)}), bf16[8,32,4096]{2,1,0:T(8,128)(2,1)S(1)}, u32[]{:S(2)}, u32[]{:S(2)}) async-start(bf16[8,32,4096]{2,1,0:T(8,128)(2,1)} %bitcast.54), calls=%async_computation | async-start | bytes 4194304 | tf_op jit(solution)/shard_map/all_to_all | solution.py:74
  101.5 0.0 all-gather.2.cloned.1.call-start
  101.5 0.1 dynamic_slice.3
  101.6 26.4 %all-to-all-done = bf16[8,32,4096]{2,1,0:T(8,128)(2,1)S(1)} async-done(((bf16[8,32,4096]{2,1,0:T(8,128)(2,1)}), bf16[8,32,4096]{2,1,0:T(8,128)(2,1)S(1)}, u32[]{:S(2)}, u32[]{:S(2)}) %all-to-all-start) | async-done | bytes 2097184 | tf_op jit(solution)/shard_map/all_to_all | solution.py:74
  128.0 9.0 %fusion.49 = f32[32,4096]{1,0:T(8,128)S(1)} fusion(bf16[8,32,4096]{2,1,0:T(8,128)(2,1)S(1)} %all-to-all-done, f32[]{:T(128)S(6)} %sub.280, f32[]{:T(128)S(6)} %sub.277, f32[]{:T(128)S(6)} %sub.274, f32[]{:T(128)S(6)} %sub.271, f32[]{:T(128)S(6)} %sub.268, f32[]{:T(128)S(6)} %sub.265, f32[]{:T(128)S(6)} %sub.262, f32[]{:T(128)S(6)} %sub.259, f32[]{:T(128)S(6)} %sub.256, ...), kind=kLoop, calls=%fused_computation.69 | loop fusion | flops 63832064 | bytes 2621504 | tf_op jit(solution)/shard_map/reduce_sum | solution.py:72
  137.0 0.0 copy-start
  137.0 0.0 copy-start.1
  137.0 0.0 copy-start.2
  137.0 0.4 reduce_sum.12
  137.5 1.2 fusion.53
  138.7 1.0 fusion.71
  139.7 1.2 reshape.128
  140.8 2.1 %fusion.64 = bf16[32,4096]{1,0:T(8,128)(2,1)} fusion(f32[32,4096]{1,0:T(8,128)} %reshape.128, f32[1,32,4096]{2,1,0:T(8,128)S(1)} %copy-done, f32[1,32,4096]{2,1,0:T(8,128)S(1)} %copy-done.1, f32[1,32,4096]{2,1,0:T(8,128)S(1)} %copy-done.2, f32[4096]{0:T(1024)S(1)} %broadcast_multiply_fusion.1), kind=kLoop, calls=%fused_computation.91 | loop fusion | flops 1966080 | bytes 2375680 | tf_op jit(solution)/shard_map/convert_element_type | solution.py:91
  143.0 0.0 all-gather.2.cloned.1.call-update
  143.0 3.2 %sort.17 = (s32[256]{0:T(256)}, s32[256]{0:T(256)S(1)}) sort(s32[256]{0:T(256)S(1)} %copy-done.6, s32[256]{0:T(256)S(1)} %iota.32), dimensions={0}, to_apply=%region_3.5 | sort | flops 2048 | bytes 4096 | tf_op jit(solution)/shard_map/jit(argsort)/sort | solution.py:92
  146.2 0.4 reshape.127
  146.6 1.4 multiply_subtract_fusion
  147.9 22.4 %all-gather.2.cloned.1.call-done = bf16[256,4096]{1,0:T(8,128)(2,1)} async-done(((bf16[32,4096]{1,0:T(8,128)(2,1)}), bf16[256,4096]{1,0:T(8,128)(2,1)}) %all-gather.2.cloned.1.call-update) | async-done | bytes 2097168 | tf_op jit(solution)/shard_map/all_gather | solution.py:91
  170.3 5.7 %gather_fusion.2 = bf16[256,4096]{1,0:T(8,128)(2,1)S(1)} fusion(bf16[256,4096]{1,0:T(8,128)(2,1)} %all-gather.2.cloned.1.call-done, s32[1024]{0:T(1024)S(1)} %pad_clamp_fusion), kind=kCustom, calls=%fused_computation.1.clone | custom fusion | bytes 4195328 | tf_op jit(solution)/shard_map/jit(_take)/gather | solution.py:93
  176.1 1.6 select_bitcast_fusion
  (21 shorter events, 0.1 us)
Async XLA Ops:
  7.2 5.6 %copy-start.5 = (s32[4096]{0:T(1024)S(1)}, s32[4096]{0:T(1024)}, u32[]{:S(2)}) copy-start(s32[4096]{0:T(1024)} %param.12) | copy-start | bytes 49156
  29.1 5.6 %copy-start.4 = (f32[16]{0:T(128)S(1)}, f32[16]{0:T(128)}, u32[]{:S(2)}) copy-start(f32[16]{0:T(128)} %param.13) | copy-start | bytes 196
  29.1 40.3 %copy-start.6 = (s32[256]{0:T(256)S(1)}, s32[256]{0:T(256)}, u32[]{:S(2)}) copy-start(s32[256]{0:T(256)} %param.14) | copy-start | bytes 3076
  97.9 30.2 %all-to-all-start = ((bf16[8,32,4096]{2,1,0:T(8,128)(2,1)}), bf16[8,32,4096]{2,1,0:T(8,128)(2,1)S(1)}, u32[]{:S(2)}, u32[]{:S(2)}) async-start(bf16[8,32,4096]{2,1,0:T(8,128)(2,1)} %bitcast.54), calls=%async_computation | async-start | bytes 4194304 | tf_op jit(solution)/shard_map/all_to_all | solution.py:74
  101.5 68.8 %all-gather.2.cloned.1.call-start = ((), (), s32[]{:S(2)}) async-start(), calls=%async_computation.1 | async-start | bytes 2359296 | tf_op jit(solution)/shard_map/all_gather | solution.py:91
  137.0 3.8 %copy-start = (f32[1,32,4096]{2,1,0:T(8,128)S(1)}, f32[1,32,4096]{2,1,0:T(8,128)}, u32[]{:S(2)}) copy-start(f32[1,32,4096]{2,1,0:T(8,128)} %param.15) | copy-start | bytes 1572868
  137.0 3.8 %copy-start.1 = (f32[1,32,4096]{2,1,0:T(8,128)S(1)}, f32[1,32,4096]{2,1,0:T(8,128)}, u32[]{:S(2)}) copy-start(f32[1,32,4096]{2,1,0:T(8,128)} %param.17) | copy-start | bytes 1572868
  137.0 3.8 %copy-start.2 = (f32[1,32,4096]{2,1,0:T(8,128)S(1)}, f32[1,32,4096]{2,1,0:T(8,128)}, u32[]{:S(2)}) copy-start(f32[1,32,4096]{2,1,0:T(8,128)} %param.16) | copy-start | bytes 1572868
  138.7 7.9 %copy-start.3 = (f32[1,32,4096]{2,1,0:T(8,128)S(1)}, f32[1,32,4096]{2,1,0:T(8,128)}, u32[]{:S(2)}) copy-start(f32[1,32,4096]{2,1,0:T(8,128)} %param.16) | copy-start | bytes 1572868
Sparse Core Ops, SparseCore 0:
  143.1 27.1 all-gather.1
where the time goes:
time: 186 us; the launch traced here: 184 us
  waiting for transfers between devices  48.8 us (26%)
  other arithmetic  43.1 us (23%)
  between operations  32.8 us (18%)
  local copies, waits for them, and re-layouts  24.9 us (13%)
  matrix products  15.8 us (8%)
  blocking collectives  15.3 us (8%)
  starting transfers between devices  3.65 us (2%)
    all_to_all x1, waiting for transfers between devices, local(): lax.all_to_all(slotted.reshape(groups, owned, slotted.shape[1]), 'dp', sp...  26.4 us
    all_gather x1, waiting for transfers between devices, local(): lax.all_gather(updated_master.astype(jnp.bfloat16), 'dp', axis=0, tiled=T...  22.4 us
    convert_element_type x1, other arithmetic, local(): (encode(rotated / block_scale[:, None], levels) + offsets).astype(jnp.bfl...  20.1 us
    dot_general x4, matrix products, square_transform(): jnp.einsum('ac,ncd,db->nab', table, folded, table, precision=lax.Precisio...  15.8 us
    pmax x1, blocking collectives, local(): block_scale = lax.pmax(peaks, 'dp') + 1e-06  15.3 us
    reduce_sum x1, other arithmetic, local(): jnp.sum(decode(lax.all_to_all(slotted.reshape(groups, owned, slotted.shap...  8.97 us
    gather x1, local copies, waits for them, and re-layouts, local(): parameters = jnp.take(gathered, inverse, axis=0)  5.74 us
    unnamed x15, local copies, waits for them, and re-layouts  5.64 us
  transfers between devices with their start and end apart: 2, of which 2 were waited for; matrix products, arithmetic and copies ran while one was open for 3% of the time, Pallas kernels for 0%

commit v1 on v0

v1 whole, which is shorter than its diff:
```python
import functools
import math

import jax
import jax.numpy as jnp
from jax import lax
from jax.experimental import pallas as pl
from jax.experimental.pallas import tpu as pltpu
from jax.sharding import PartitionSpec as P

MESH = pl.DeviceIdType.MESH
adam_epsilon = 1e-08
learning_rate = 0.02
weight_decay = 0.1
first_decay = 0.9
second_decay = 0.95
dither_steps = 256.0
CHUNKS = 4
LANES = 128
TILE = 256
VMEM_LIMIT = 60 * 1024 * 1024


def hadamard(edge, scale):
    rows = lax.broadcasted_iota(jnp.int32, (edge, edge), 0)
    columns = lax.broadcasted_iota(jnp.int32, (edge, edge), 1)
    common = rows & columns
    parity = jnp.zeros((edge, edge), jnp.int32)
    for bit in range(edge.bit_length() - 1):
        parity = parity + ((common >> bit) & 1)
    return ((1 - 2 * (parity & 1)).astype(jnp.float32) * scale).astype(jnp.bfloat16)


def exact_dot(x, table):
    high = x.astype(jnp.bfloat16)
    rest = x - high.astype(jnp.float32)
    middle = rest.astype(jnp.bfloat16)
    low = (rest - middle.astype(jnp.float32)).astype(jnp.bfloat16)
    dot = functools.partial(jnp.dot, preferred_element_type=jnp.float32)
    return dot(high, table) + (dot(middle, table) + dot(low, table))


def butterflies(pieces):
    pieces = list(pieces)
    step = 1
    while step < len(pieces):
        for i in range(len(pieces)):
            if not i & step:
                a, b = pieces[i], pieces[i + step]
                pieces[i], pieces[i + step] = a + b, a - b
        step *= 2
    return pieces


def transform(pieces, table):
    rows = pieces[0].shape[0]
    turned = exact_dot(jnp.concatenate(pieces, axis=0), table)
    return butterflies([turned[c * rows : (c + 1) * rows] for c in range(len(pieces))])


def lookup(table, index):
    return jnp.take_along_axis(
        jnp.broadcast_to(table, index.shape), index, axis=1, mode="promise_in_bounds"
    )


def level_rows(levels_ref, count):
    lane = lax.broadcasted_iota(jnp.int32, (1, LANES), 1)
    here = jnp.zeros((1, LANES), jnp.float32)
    after = jnp.zeros((1, LANES), jnp.float32)
    for k in range(count):
        here = jnp.where(lane == k, levels_ref[k], here)
        after = jnp.where(lane == k, levels_ref[min(k + 1, count - 1)], after)
    return lane, here, after


def step_kernel(
    n, grad_hbm, dith_hbm, sign_ref, levels_ref, layout_ref, mst_hbm, fm_hbm, sm_hbm,
    um_hbm, uf_hbm, us_hbm, gall,
    x, dith, rot, pmat, hmat, flip, peaks, pk_send, pk_recv, symt, sym, symr, sums,
    mst, fm, sm, um, uf, us, pr,
    load_sem, dith_sem, side_sem, pks_sem, pkr_sem, as_sem, ar_sem, gs_sem, gr_sem, rs_sem, rr_sem,
):
    me = lax.axis_index("dp")
    blocks, size = x.shape
    own = blocks // n
    tiles = size // TILE
    per = tiles // CHUNKS
    rows = blocks // load_sem.shape[0]
    chips = n // 2
    chip, core = me // 2, lax.rem(me, 2)
    partner = chip * 2 + 1 - core
    count = levels_ref.shape[0]

    def load(i):
        part = pl.ds(pl.multiple_of(i * rows, rows), rows)
        return pltpu.make_async_copy(grad_hbm.at[part], x.at[part], load_sem.at[i])

    for i in range(blocks // rows):
        load(i).start()

    def load_dither(t):
        return pltpu.make_async_copy(
            dith_hbm.at[:, t * TILE : (t + 1) * TILE], dith.at[t], dith_sem.at[t]
        )

    for t in range(tiles):
        load_dither(t).start()
    sides = [
        pltpu.make_async_copy(src, dst, side_sem.at[i])
        for i, (src, dst) in enumerate(((mst_hbm, mst), (fm_hbm, fm), (sm_hbm, sm)))
    ]
    for side in sides:
        side.start()

    barrier = pltpu.get_barrier_semaphore()

    def greet(k, carry):
        pl.semaphore_signal(barrier, inc=1, device_id={"dp": lax.rem(me + k, n)}, device_id_type=MESH)
        return carry

    lax.fori_loop(1, n, greet, 0)

    flip[...] = (1 - 2 * sign_ref[...]).astype(jnp.float32)
    hmat[...] = hadamard(TILE, 1.0 / math.isqrt(size))
    block_row = lax.broadcasted_iota(jnp.int32, (blocks, blocks), 0)
    block_col = lax.broadcasted_iota(jnp.int32, (blocks, blocks), 1)
    turned_p = (block_row == layout_ref[...]).astype(jnp.float32)
    pmat[...] = turned_p.T

    @pl.loop(0, blocks // rows)
    def _(i):
        load(i).wait()
        part = pl.ds(pl.multiple_of(i * rows, rows), rows)
        pieces = [x[part, c * TILE : (c + 1) * TILE] * flip[:, c * TILE : (c + 1) * TILE] for c in range(tiles)]
        pieces = transform(pieces, hmat[...])
        top = jnp.abs(pieces[0])
        for c in range(tiles):
            rot[c, part] = pieces[c]
            top = jnp.maximum(top, jnp.abs(pieces[c]))
        peaks[part] = jnp.broadcast_to(jnp.max(top, axis=1, keepdims=True), (rows, LANES))

    eye = block_row == block_col
    peak_row = jnp.max(jnp.where(eye, peaks[:, :1], 0.0), axis=0, keepdims=True)
    pk_send[...] = jnp.broadcast_to(peak_row, pk_send.shape)
    pl.semaphore_wait(barrier, n - 1)

    def peak_copy(k):
        return pltpu.make_async_remote_copy(
            src_ref=pk_send, dst_ref=pk_recv.at[k], send_sem=pks_sem.at[k], recv_sem=pkr_sem.at[k],
            device_id={"dp": lax.rem(me + k, n)}, device_id_type=MESH,
        )

    def run(first, last, do):
        def body(k, carry):
            do(k)
            return carry
        lax.fori_loop(first, last, body, 0)

    run(1, n, lambda k: peak_copy(k).start())

    lane, here, after = level_rows(levels_ref, count)
    gap = after - here
    inside = lane < count - 1
    slope = jnp.where(inside, 1.0 / jnp.where(inside, gap, 1.0), 0.0)
    base = jnp.where(inside, lane.astype(jnp.float32) - here * slope, float(count - 1))
    delta = jnp.where(inside, gap, 0.0)
    start = jnp.where(inside, here - delta * lane.astype(jnp.float32), here)
    half_cells = LANES // 2
    edge = lane.astype(jnp.float32) / half_cells - 1.0
    first_index = jnp.zeros((1, LANES), jnp.int32)
    kink = jnp.full((1, LANES), 4.0, jnp.float32)
    for k in range(count - 2, 0, -1):
        first_index = first_index + (edge >= levels_ref[k]).astype(jnp.int32)
        kink = jnp.where(edge < levels_ref[k], levels_ref[k], kink)

    run(1, n, lambda k: peak_copy(k).wait_recv())
    best = pk_send[...]
    for k in range(1, n):
        best = jnp.maximum(best, pk_recv[k])
    scale_row = best[:1] + 1e-06
    scale_col = jnp.max(jnp.where(eye, scale_row, 0.0), axis=1, keepdims=True)
    peaks[...] = jnp.broadcast_to(1.0 / scale_col, peaks.shape)
    mine = pl.ds(pl.multiple_of(me * own, own), own)
    slot_scale = jnp.max(pmat[mine] * scale_row, axis=1, keepdims=True)
    perm = pmat[...].astype(jnp.bfloat16)

    def symbol_copy(q, k):
        peer = lax.rem(me + k, n)
        part = pl.ds(q * per, per)
        return pltpu.make_async_remote_copy(
            src_ref=sym.at[part, peer], dst_ref=symr.at[part, me],
            send_sem=as_sem.at[q, k], recv_sem=ar_sem.at[q, k],
            device_id={"dp": peer}, device_id_type=MESH,
        )

    group = 32
    for t in range(tiles):
        load_dither(t).wait()

    def encode(q):
        def tile(s, carry):
            t = q * per + s
            for r in range(blocks // group):
                part = slice(r * group, (r + 1) * group)
                inverse = peaks[part]
                for h in range(TILE // LANES):
                    side = slice(h * LANES, (h + 1) * LANES)
                    ratio = rot[t, part, side] * inverse
                    cell = jnp.minimum((ratio * half_cells + half_cells).astype(jnp.int32), LANES - 1)
                    cell = jnp.maximum(cell, 0)
                    at = lookup(first_index, cell) + (ratio >= lookup(kink, cell)).astype(jnp.int32)
                    relaxed = lookup(base, at) + lookup(slope, at) * ratio
                    offset = dith[t, part, side].astype(jnp.float32) * (1.0 / dither_steps) + (0.5 / dither_steps - 0.5)
                    symt[part, side] = (relaxed + offset).astype(jnp.bfloat16)
            moved = jnp.dot(perm, symt[...], preferred_element_type=jnp.float32).astype(jnp.bfloat16)
            sym[t] = moved.reshape(n, own, TILE)
            symr[t, me] = sym[t, me]
            return carry

        lax.fori_loop(0, per, tile, 0)
        run(1, n, lambda k: symbol_copy(q, k).start())

    run(0, CHUNKS, encode)

    def decode(q):
        run(1, n, lambda k: symbol_copy(q, k).wait_recv())

        def tile(s, carry):
            t = q * per + s
            for h in range(TILE // LANES):
                side = slice(h * LANES, (h + 1) * LANES)
                total = jnp.zeros((own, LANES), jnp.float32)
                for source in range(n):
                    value = symr[t, source, :, side].astype(jnp.float32)
                    value = jnp.clip(value, 0.0, float(count - 1))
                    at = value.astype(jnp.int32)
                    total = total + (lookup(start, at) + lookup(delta, at) * value)
                sums[t, :, side] = total * slot_scale
            return carry

        lax.fori_loop(0, per, tile, 0)

    run(0, CHUNKS, decode)

    for side in sides:
        side.wait()
    grads = transform([sums[c] for c in range(tiles)], hmat[...])
    for c in range(tiles):
        cut = slice(c * TILE, (c + 1) * TILE)
        grad = grads[c] * flip[:, cut]
        master = mst[:, cut]
        first = first_decay * fm[:, cut] + (1.0 - first_decay) * grad
        second = second_decay * sm[:, cut] + (1.0 - second_decay) * grad * grad
        fresh = master - learning_rate * (first / (jnp.sqrt(second) + adam_epsilon) + weight_decay * master)
        uf[:, cut] = first
        us[:, cut] = second
        um[:, cut] = fresh
        pr[:, cut] = fresh.astype(jnp.bfloat16)

    def gather_copy(c):
        peer = lax.rem(chip + c, chips) * 2 + core
        return pltpu.make_async_remote_copy(
            src_ref=pr, dst_ref=gall.at[me], send_sem=gs_sem.at[c], recv_sem=gr_sem.at[c],
            device_id={"dp": peer}, device_id_type=MESH,
        )

    def relay_copy(c):
        source = lax.rem(chip + chips - c, chips) * 2 + core
        return pltpu.make_async_remote_copy(
            src_ref=gall.at[source], dst_ref=gall.at[source], send_sem=rs_sem.at[c], recv_sem=rr_sem.at[c],
            device_id={"dp": partner}, device_id_type=MESH,
        )

    own_relay = pltpu.make_async_remote_copy(
        src_ref=pr, dst_ref=gall.at[me], send_sem=rs_sem.at[0], recv_sem=rr_sem.at[0],
        device_id={"dp": partner}, device_id_type=MESH,
    )
    run(1, chips, lambda c: gather_copy(c).start())
    own_relay.start()
    outs = [
        pltpu.make_async_copy(src, dst, side_sem.at[3 + i])
        for i, (src, dst) in enumerate(((um, um_hbm), (uf, uf_hbm), (us, us_hbm), (pr, gall.at[me])))
    ]
    for out in outs:
        out.start()

    def relay(c):
        gather_copy(c).wait_recv()
        relay_copy(c).start()

    run(1, chips, relay)
    own_relay.wait()
    run(1, chips, lambda c: relay_copy(c).wait())
    run(1, chips, lambda c: gather_copy(c).wait_send())
    run(1, n, lambda k: peak_copy(k).wait_send())

    def drain(q):
        run(1, n, lambda k: symbol_copy(q, k).wait_send())

    run(0, CHUNKS, drain)
    for out in outs:
        out.wait()


def spread_kernel(layout_ref, gall_ref, um_in, uf_in, us_in, um_out, uf_out, us_out, out_ref):
    blocks = layout_ref.shape[1]
    rows = lax.broadcasted_iota(jnp.int32, (blocks, blocks), 0)
    table = (rows == layout_ref[...]).astype(jnp.float32).astype(jnp.bfloat16)
    out_ref[...] = jnp.dot(table, gall_ref[...], preferred_element_type=jnp.float32).astype(jnp.bfloat16)
    um_out[...] = um_in[...]
    uf_out[...] = uf_in[...]
    us_out[...] = us_in[...]


def local(n, gradient, dither, sign_bits, levels, layout, master, first_moment, second_moment):
    blocks, size = gradient.shape[2:]
    own = blocks // n
    tiles = size // TILE
    row_chunks = 8
    f32, bf16 = jnp.float32, jnp.bfloat16
    hbm = pl.BlockSpec(memory_space=pl.ANY)
    vmem = pl.BlockSpec(memory_space=pltpu.VMEM)
    dma = pltpu.SemaphoreType.DMA
    layout_row = layout.reshape(1, blocks)
    shard = jax.ShapeDtypeStruct((own, size), f32)
    um, uf, us, gall = pl.pallas_call(
        functools.partial(step_kernel, n),
        out_shape=(shard, shard, shard, jax.ShapeDtypeStruct((n, own, size), bf16)),
        in_specs=[hbm, hbm, vmem, pl.BlockSpec(memory_space=pltpu.SMEM), vmem, hbm, hbm, hbm],
        out_specs=(hbm, hbm, hbm, hbm),
        scratch_shapes=[
            pltpu.VMEM((blocks, size), f32),
            pltpu.VMEM((tiles, blocks, TILE), jnp.int32),
            pltpu.VMEM((tiles, blocks, TILE), f32),
            pltpu.VMEM((blocks, blocks), f32),
            pltpu.VMEM((TILE, TILE), bf16),
            pltpu.VMEM((1, size), f32),
            pltpu.VMEM((blocks, LANES), f32),
            pltpu.VMEM((8, blocks), f32),
            pltpu.VMEM((n, 8, blocks), f32),
            pltpu.VMEM((blocks, TILE), bf16),
            pltpu.VMEM((tiles, n, own, TILE), bf16),
            pltpu.VMEM((tiles, n, own, TILE), bf16),
            pltpu.VMEM((tiles, own, TILE), f32),
            *[pltpu.VMEM((own, size), f32)] * 6,
            pltpu.VMEM((own, size), bf16),
            dma((row_chunks,)),
            dma((tiles,)),
            dma((7,)),
            dma((n,)),
            dma((n,)),
            dma((CHUNKS, n)),
            dma((CHUNKS, n)),
            dma((n // 2,)),
            dma((n // 2,)),
            dma((n // 2,)),
            dma((n // 2,)),
        ],
        compiler_params=pltpu.CompilerParams(
            collective_id=0, has_side_effects=True, vmem_limit_bytes=VMEM_LIMIT
        ),
    )(
        gradient[0, 0], dither[0, 0], sign_bits.reshape(1, size), levels, layout_row,
        master[0], first_moment[0], second_moment[0],
    )
    width = size // 4
    wide = pl.BlockSpec((blocks, width), lambda i: (0, i))
    narrow = pl.BlockSpec((own, width), lambda i: (0, i))
    um, uf, us, parameters = pl.pallas_call(
        spread_kernel,
        grid=(4,),
        out_shape=(shard, shard, shard, jax.ShapeDtypeStruct((blocks, size), bf16)),
        in_specs=[pl.BlockSpec((1, blocks), lambda i: (0, 0)), wide, narrow, narrow, narrow],
        out_specs=(narrow, narrow, narrow, wide),
    )(layout_row, gall.reshape(blocks, size), um, uf, us)
    return um[None], uf[None], us[None], parameters[None]


def solution(mesh):
    slots = P("section", "dp", None)
    streams = P("section", "dp", None, None)
    return jax.shard_map(
        functools.partial(local, mesh.shape["dp"]),
        mesh=mesh,
        in_specs=(streams, streams, P(), P(), P(), slots, slots, slots),
        out_specs=(slots, slots, slots, P("section", None, None)),
        check_vma=False,
    )
```

time: 186 us -> 66.2 us (0.36)
  Pallas kernels: 0 us -> 65.3 us
  waiting for transfers between devices: 48.8 us -> 0 us
  other arithmetic: 43.1 us -> 0 us
  between operations: 32.8 us -> 0.64 us
  local copies, waits for them, and re-layouts: 24.9 us -> 0 us
  matrix products: 15.8 us -> 0 us
  blocking collectives: 15.3 us -> 0 us
  starting transfers between devices: 3.65 us -> 0 us
    pallas_call x0 -> x2, Pallas kernels: none -> 65.3 us  [the longest x1 60.5 us: local(): pl.pallas_call(functools.partial(step_kernel, n), out_shape=(shard, shard...]
    all_to_all x1 -> x0, waiting for transfers between devices: 26.4 us -> none  [local(): lax.all_to_all(slotted.reshape(groups, owned, slotted.shape[1]), 'dp', sp...]
    all_gather x1 -> x0, waiting for transfers between devices: 22.4 us -> none  [local(): lax.all_gather(updated_master.astype(jnp.bfloat16), 'dp', axis=0, tiled=T...]
    convert_element_type x3 -> x0, other arithmetic: 22.2 us -> none  [the longest x1 20.1 us: local(): (encode(rotated / block_scale[:, None], levels) + offsets).astype(jnp.bfl...]
    dot_general x4 -> x0, matrix products: 15.8 us -> none  [square_transform(): jnp.einsum('ac,ncd,db->nab', table, folded, table, precision=lax.Precisio...]
    pmax x1 -> x0, blocking collectives: 15.3 us -> none  [local(): block_scale = lax.pmax(peaks, 'dp') + 1e-06]
    gather x3 -> x0, local copies, waits for them, and re-layouts: 10.9 us -> none  [the longest x1 5.74 us: local(): parameters = jnp.take(gathered, inverse, axis=0)]
    reduce_sum x1 -> x0, other arithmetic: 8.97 us -> none  [local(): jnp.sum(decode(lax.all_to_all(slotted.reshape(groups, owned, slotted.shap...]
  transfers between devices with their start and end apart: 2 -> 0, of which waited for: 2 -> 0; matrix products, arithmetic and copies ran while one was open for 3% -> 0% of each run, Pallas kernels for 0% -> 0%
where the time goes in v1:
time: 66.2 us; the launch traced here: 65.9 us
  Pallas kernels  65.3 us (99%)
    pallas_call x1, Pallas kernels, local(): pl.pallas_call(functools.partial(step_kernel, n), out_shape=(shard, shard...  60.5 us
    pallas_call x1, Pallas kernels, local(): pl.pallas_call(spread_kernel, grid=(4,), out_shape=(shard, shard, shard,...  4.78 us

profile of v1, /device:TPU:0, one launch (start us, length us, event | category | flops | bytes accessed | tf_op | source)
XLA Modules:
  0.0 65.9 jit_solution(6002869140011272843)
XLA Ops:
  0.6 60.5 %shard_map.111 = (f32[32,4096]{1,0:T(8,128)}, f32[32,4096]{1,0:T(8,128)}, f32[32,4096]{1,0:T(8,128)}, bf16[8,32,4096]{2,1,0:T(8,128)(2,1)}) custom-call(f32[256,4096]{1,0:T(8,128)} %bitcast.12, s32[256,4096]{1,0:T(8,128)} %bitcast.13, s32[1,4096]{1,0:T(1,128)} %bitcast.18, f32[16]{0:T(128)} %levels_ref.1, s32[1,256]{1,0:T(1,128)} %bitcast.19, ...), custom_call_target="tpu_custom_call" | custom-call | tf_op jit(solution)/shard_map/pallas_call | solution.py:327
  61.2 4.8 %shard_map.112 = (f32[32,4096]{1,0:T(8,128)}, f32[32,4096]{1,0:T(8,128)}, f32[32,4096]{1,0:T(8,128)}, bf16[256,4096]{1,0:T(8,128)(2,1)}) custom-call(s32[1,256]{1,0:T(1,128)} %bitcast.20, bf16[256,4096]{1,0:T(8,128)(2,1)} %bitcast.14, f32[32,4096]{1,0:T(8,128)} %get-tuple-element.13.um_in, f32[32,4096]{1,0:T(8,128)} %get-tuple-element.14.uf_in, ...), custom_call_target="tpu_custom_call" | custom-call | tf_op jit(solution)/shard_map/pallas_call | solution.py:370

commit v2 on v1

--- a/solution.py
+++ b/solution.py
@@ -15,7 +15,7 @@
 first_decay = 0.9
 second_decay = 0.95
 dither_steps = 256.0
-CHUNKS = 4
+CHUNKS = 8
 LANES = 128
 TILE = 256
 VMEM_LIMIT = 60 * 1024 * 1024
@@ -62,6 +62,20 @@
     return jnp.take_along_axis(
         jnp.broadcast_to(table, index.shape), index, axis=1, mode="promise_in_bounds"
     )
+
+
+def piecewise(value, spots, bases, slopes):
+    base = jnp.full(value.shape, bases[0], jnp.float32)
+    slope = jnp.full(value.shape, slopes[0], jnp.float32)
+    for spot, next_base, next_slope in zip(spots, bases[1:], slopes[1:]):
+        past = value >= spot
+        base = jnp.where(past, next_base, base)
+        slope = jnp.where(past, next_slope, slope)
+    return base + slope * value
+
+
+def slot_groups(own):
+    return 2 if own % 32 == 0 else 1
 
 
 def level_rows(levels_ref, count):
@@ -91,6 +105,8 @@
     chip, core = me // 2, lax.rem(me, 2)
     partner = chip * 2 + 1 - core
     count = levels_ref.shape[0]
+    groups = slot_groups(own)
+    half = own // groups
 
     def load(i):
         part = pl.ds(pl.multiple_of(i * rows, rows), rows)
@@ -160,19 +176,15 @@
     run(1, n, lambda k: peak_copy(k).start())
 
     lane, here, after = level_rows(levels_ref, count)
-    gap = after - here
     inside = lane < count - 1
-    slope = jnp.where(inside, 1.0 / jnp.where(inside, gap, 1.0), 0.0)
-    base = jnp.where(inside, lane.astype(jnp.float32) - here * slope, float(count - 1))
-    delta = jnp.where(inside, gap, 0.0)
+    delta = jnp.where(inside, after - here, 0.0)
     start = jnp.where(inside, here - delta * lane.astype(jnp.float32), here)
-    half_cells = LANES // 2
-    edge = lane.astype(jnp.float32) / half_cells - 1.0
-    first_index = jnp.zeros((1, LANES), jnp.int32)
-    kink = jnp.full((1, LANES), 4.0, jnp.float32)
-    for k in range(count - 2, 0, -1):
-        first_index = first_index + (edge >= levels_ref[k]).astype(jnp.int32)
-        kink = jnp.where(edge < levels_ref[k], levels_ref[k], kink)
+    spots = [levels_ref[k] for k in range(1, count - 1)]
+    gaps = [levels_ref[k + 1] - levels_ref[k] for k in range(count - 1)]
+    slopes = [1.0 / gap for gap in gaps]
+    bases = [float(k) - levels_ref[k] * slopes[k] for k in range(count - 1)]
+    whole = [float(k) for k in range(1, count - 1)]
+    starts = [levels_ref[k] - gaps[k] * float(k) for k in range(count - 1)]
 
     run(1, n, lambda k: peak_copy(k).wait_recv())
     best = pk_send[...]
@@ -185,12 +197,13 @@
     slot_scale = jnp.max(pmat[mine] * scale_row, axis=1, keepdims=True)
     perm = pmat[...].astype(jnp.bfloat16)
 
-    def symbol_copy(q, k):
+    def symbol_copy(g, q, k):
         peer = lax.rem(me + k, n)
         part = pl.ds(q * per, per)
+        slots = pl.ds(g * half, half)
         return pltpu.make_async_remote_copy(
-            src_ref=sym.at[part, peer], dst_ref=symr.at[part, me],
-            send_sem=as_sem.at[q, k], recv_sem=ar_sem.at[q, k],
+            src_ref=sym.at[part, peer, slots], dst_ref=symr.at[part, me, slots],
+            send_sem=as_sem.at[g, q, k], recv_sem=ar_sem.at[g, q, k],
             device_id={"dp": peer}, device_id_type=MESH,
         )
 
@@ -207,10 +220,7 @@
                 for h in range(TILE // LANES):
                     side = slice(h * LANES, (h + 1) * LANES)
                     ratio = rot[t, part, side] * inverse
-                    cell = jnp.minimum((ratio * half_cells + half_cells).astype(jnp.int32), LANES - 1)
-                    cell = jnp.maximum(cell, 0)
-                    at = lookup(first_index, cell) + (ratio >= lookup(kink, cell)).astype(jnp.int32)
-                    relaxed = lookup(base, at) + lookup(slope, at) * ratio
+                    relaxed = piecewise(ratio, spots, bases, slopes)
                     offset = dith[t, part, side].astype(jnp.float32) * (1.0 / dither_steps) + (0.5 / dither_steps - 0.5)
                     symt[part, side] = (relaxed + offset).astype(jnp.bfloat16)
             moved = jnp.dot(perm, symt[...], preferred_element_type=jnp.float32).astype(jnp.bfloat16)
@@ -219,65 +229,77 @@
             return carry
 
         lax.fori_loop(0, per, tile, 0)
-        run(1, n, lambda k: symbol_copy(q, k).start())
+        run(1, n, lambda k: symbol_copy(0, q, k).start())
 
     run(0, CHUNKS, encode)
-
-    def decode(q):
-        run(1, n, lambda k: symbol_copy(q, k).wait_recv())
+    for g in range(1, groups):
+        run(0, CHUNKS, lambda q: run(1, n, lambda k: symbol_copy(g, q, k).start()))
+
+    def decode(g, q):
+        run(1, n, lambda k: symbol_copy(g, q, k).wait_recv())
+        slots = slice(g * half, (g + 1) * half)
 
         def tile(s, carry):
             t = q * per + s
             for h in range(TILE // LANES):
                 side = slice(h * LANES, (h + 1) * LANES)
-                total = jnp.zeros((own, LANES), jnp.float32)
+                total = jnp.zeros((half, LANES), jnp.float32)
                 for source in range(n):
-                    value = symr[t, source, :, side].astype(jnp.float32)
+                    value = symr[t, source, slots, side].astype(jnp.float32)
                     value = jnp.clip(value, 0.0, float(count - 1))
-                    at = value.astype(jnp.int32)
-                    total = total + (lookup(start, at) + lookup(delta, at) * value)
-                sums[t, :, side] = total * slot_scale
+                    if source % 2:
+                        total = total + piecewise(value, whole, starts, gaps)
+                    else:
+                        at = value.astype(jnp.int32)
+                        total = total + (lookup(start, at) + lookup(delta, at) * value)
+                sums[t, slots, side] = total * slot_scale[slots]
             return carry
 
         lax.fori_loop(0, per, tile, 0)
 
-    run(0, CHUNKS, decode)
+    def gather_copy(g, c):
+        peer = lax.rem(chip + c, chips) * 2 + core
+        slots = pl.ds(g * half, half)
+        return pltpu.make_async_remote_copy(
+            src_ref=pr.at[slots], dst_ref=gall.at[me, slots], send_sem=gs_sem.at[g, c], recv_sem=gr_sem.at[g, c],
+            device_id={"dp": peer}, device_id_type=MESH,
+        )
+
+    def relay_copy(g, c):
+        source = lax.rem(chip + chips - c, chips) * 2 + core
+        slots = pl.ds(g * half, half)
+        return pltpu.make_async_remote_copy(
+            src_ref=gall.at[source, slots], dst_ref=gall.at[source, slots],
+            send_sem=rs_sem.at[g, c], recv_sem=rr_sem.at[g, c],
+            device_id={"dp": partner}, device_id_type=MESH,
+        )
+
+    def own_relay(g):
+        slots = pl.ds(g * half, half)
+        return pltpu.make_async_remote_copy(
+            src_ref=pr.at[slots], dst_ref=gall.at[me, slots], send_sem=rs_sem.at[g, 0], recv_sem=rr_sem.at[g, 0],
+            device_id={"dp": partner}, device_id_type=MESH,
+        )
 
     for side in sides:
         side.wait()
-    grads = transform([sums[c] for c in range(tiles)], hmat[...])
-    for c in range(tiles):
-        cut = slice(c * TILE, (c + 1) * TILE)
-        grad = grads[c] * flip[:, cut]
-        master = mst[:, cut]
-        first = first_decay * fm[:, cut] + (1.0 - first_decay) * grad
-        second = second_decay * sm[:, cut] + (1.0 - second_decay) * grad * grad
-        fresh = master - learning_rate * (first / (jnp.sqrt(second) + adam_epsilon) + weight_decay * master)
-        uf[:, cut] = first
-        us[:, cut] = second
-        um[:, cut] = fresh
-        pr[:, cut] = fresh.astype(jnp.bfloat16)
-
-    def gather_copy(c):
-        peer = lax.rem(chip + c, chips) * 2 + core
-        return pltpu.make_async_remote_copy(
-            src_ref=pr, dst_ref=gall.at[me], send_sem=gs_sem.at[c], recv_sem=gr_sem.at[c],
-            device_id={"dp": peer}, device_id_type=MESH,
-        )
-
-    def relay_copy(c):
-        source = lax.rem(chip + chips - c, chips) * 2 + core
-        return pltpu.make_async_remote_copy(
-            src_ref=gall.at[source], dst_ref=gall.at[source], send_sem=rs_sem.at[c], recv_sem=rr_sem.at[c],
-            device_id={"dp": partner}, device_id_type=MESH,
-        )
-
-    own_relay = pltpu.make_async_remote_copy(
-        src_ref=pr, dst_ref=gall.at[me], send_sem=rs_sem.at[0], recv_sem=rr_sem.at[0],
-        device_id={"dp": partner}, device_id_type=MESH,
-    )
-    run(1, chips, lambda c: gather_copy(c).start())
-    own_relay.start()
+    for g in range(groups):
+        run(0, CHUNKS, functools.partial(decode, g))
+        slots = slice(g * half, (g + 1) * half)
+        grads = transform([sums[c, slots] for c in range(tiles)], hmat[...])
+        for c in range(tiles):
+            cut = slice(c * TILE, (c + 1) * TILE)
+            grad = grads[c] * flip[:, cut]
+            master = mst[slots, cut]
+            first = first_decay * fm[slots, cut] + (1.0 - first_decay) * grad
+            second = second_decay * sm[slots, cut] + (1.0 - second_decay) * grad * grad
+            fresh = master - learning_rate * (first / (jnp.sqrt(second) + adam_epsilon) + weight_decay * master)
+            uf[slots, cut] = first
+            us[slots, cut] = second
+            um[slots, cut] = fresh
+            pr[slots, cut] = fresh.astype(jnp.bfloat16)
+        run(1, chips, lambda c: gather_copy(g, c).start())
+        own_relay(g).start()
     outs = [
         pltpu.make_async_copy(src, dst, side_sem.at[3 + i])
         for i, (src, dst) in enumerate(((um, um_hbm), (uf, uf_hbm), (us, us_hbm), (pr, gall.at[me])))
@@ -285,20 +307,18 @@
     for out in outs:
         out.start()
 
-    def relay(c):
-        gather_copy(c).wait_recv()
-        relay_copy(c).start()
-
-    run(1, chips, relay)
-    own_relay.wait()
-    run(1, chips, lambda c: relay_copy(c).wait())
-    run(1, chips, lambda c: gather_copy(c).wait_send())
+    for g in range(groups):
+        def relay(c):
+            gather_copy(g, c).wait_recv()
+            relay_copy(g, c).start()
+
+        run(1, chips, relay)
+    for g in range(groups):
+        own_relay(g).wait()
+        run(1, chips, lambda c: relay_copy(g, c).wait())
+        run(1, chips, lambda c: gather_copy(g, c).wait_send())
+        run(0, CHUNKS, lambda q: run(1, n, lambda k: symbol_copy(g, q, k).wait_send()))
     run(1, n, lambda k: peak_copy(k).wait_send())
-
-    def drain(q):
-        run(1, n, lambda k: symbol_copy(q, k).wait_send())
-
-    run(0, CHUNKS, drain)
     for out in outs:
         out.wait()
 
@@ -318,6 +338,7 @@
     own = blocks // n
     tiles = size // TILE
     row_chunks = 8
+    groups = slot_groups(own)
     f32, bf16 = jnp.float32, jnp.bfloat16
     hbm = pl.BlockSpec(memory_space=pl.ANY)
     vmem = pl.BlockSpec(memory_space=pltpu.VMEM)
@@ -350,12 +371,9 @@
             dma((7,)),
             dma((n,)),
             dma((n,)),
-            dma((CHUNKS, n)),
-            dma((CHUNKS, n)),
-            dma((n // 2,)),
-            dma((n // 2,)),
-            dma((n // 2,)),
-            dma((n // 2,)),
+            dma((groups, CHUNKS, n)),
+            dma((groups, CHUNKS, n)),
+            *[dma((groups, n // 2))] * 4,
         ],
         compiler_params=pltpu.CompilerParams(
             collective_id=0, has_side_effects=True, vmem_limit_bytes=VMEM_LIMIT
@@ -364,12 +382,12 @@
         gradient[0, 0], dither[0, 0], sign_bits.reshape(1, size), levels, layout_row,
         master[0], first_moment[0], second_moment[0],
     )
-    width = size // 4
+    width = size // 8
     wide = pl.BlockSpec((blocks, width), lambda i: (0, i))
     narrow = pl.BlockSpec((own, width), lambda i: (0, i))
     um, uf, us, parameters = pl.pallas_call(
         spread_kernel,
-        grid=(4,),
+        grid=(8,),
         out_shape=(shard, shard, shard, jax.ShapeDtypeStruct((blocks, size), bf16)),
         in_specs=[pl.BlockSpec((1, blocks), lambda i: (0, 0)), wide, narrow, narrow, narrow],
         out_specs=(narrow, narrow, narrow, wide),

time: 66.2 us -> 61.7 us (0.932)
  Pallas kernels: 65.3 us -> 60.8 us
    pallas_call x1, Pallas kernels: 60.5 us -> 54 us  [local(): pl.pallas_call(functools.partial(step_kernel, n), out_shape=(shard, shard...]
    pallas_call x1, Pallas kernels: 4.78 us -> 6.78 us  [local(): pl.pallas_call(spread_kernel, grid=(8,), out_shape=(shard, shard, shard,...]
where the time goes in v2:
time: 61.7 us; the launch traced here: 61.4 us
  Pallas kernels  60.8 us (99%)
  between operations  0.64 us (1%)
    pallas_call x1, Pallas kernels, local(): pl.pallas_call(functools.partial(step_kernel, n), out_shape=(shard, shard...  54 us
    pallas_call x1, Pallas kernels, local(): pl.pallas_call(spread_kernel, grid=(8,), out_shape=(shard, shard, shard,...  6.78 us

profile of v2, /device:TPU:0, one launch (start us, length us, event | category | flops | bytes accessed | tf_op | source)
XLA Modules:
  0.0 61.4 jit_solution(184200723379992923)
XLA Ops:
  0.6 54.0 %shard_map.111 = (f32[32,4096]{1,0:T(8,128)}, f32[32,4096]{1,0:T(8,128)}, f32[32,4096]{1,0:T(8,128)}, bf16[8,32,4096]{2,1,0:T(8,128)(2,1)}) custom-call(f32[256,4096]{1,0:T(8,128)} %bitcast.12, s32[256,4096]{1,0:T(8,128)} %bitcast.13, s32[1,4096]{1,0:T(1,128)} %bitcast.18, f32[16]{0:T(128)} %levels_ref.1, s32[1,256]{1,0:T(1,128)} %bitcast.19, ...), custom_call_target="tpu_custom_call" | custom-call | tf_op jit(solution)/shard_map/pallas_call | solution.py:348
  54.7 6.8 %shard_map.112 = (f32[32,4096]{1,0:T(8,128)}, f32[32,4096]{1,0:T(8,128)}, f32[32,4096]{1,0:T(8,128)}, bf16[256,4096]{1,0:T(8,128)(2,1)}) custom-call(s32[1,256]{1,0:T(1,128)} %bitcast.20, bf16[256,4096]{1,0:T(8,128)(2,1)} %bitcast.14, f32[32,4096]{1,0:T(8,128)} %get-tuple-element.13.um_in, f32[32,4096]{1,0:T(8,128)} %get-tuple-element.14.uf_in, ...), custom_call_target="tpu_custom_call" | custom-call | tf_op jit(solution)/shard_map/pallas_call | solution.py:388

commit v3 on v2

--- a/solution.py
+++ b/solution.py
@@ -281,6 +281,37 @@
             device_id={"dp": partner}, device_id_type=MESH,
         )
 
+    square = chips == 4
+    near = chip + 1 - 2 * lax.rem(chip, 2)
+    across = lax.rem(chip + 2, 4)
+    corner = lax.rem(near + 2, 4)
+    left, right, full = (0, size // 2), (size // 2, size // 2), (0, size)
+
+    def shard_copy(g, kind, source, columns, to_chip, send, recv):
+        at = gall.at[source, pl.ds(g * half, half), pl.ds(*columns)]
+        own_part = pr.at[pl.ds(g * half, half), pl.ds(*columns)]
+        return pltpu.make_async_remote_copy(
+            src_ref=own_part if source is me else at, dst_ref=at,
+            send_sem=send.at[g, kind], recv_sem=recv.at[g, kind],
+            device_id={"dp": to_chip}, device_id_type=MESH,
+        )
+
+    def square_copies(g):
+        to_near, to_across = near * 2 + core, across * 2 + core
+        hops = [
+            shard_copy(g, 0, me, left, to_near, gs_sem, gr_sem),
+            shard_copy(g, 1, me, right, to_across, gs_sem, gr_sem),
+            shard_copy(g, 2, me, right, to_near, gs_sem, gr_sem),
+            shard_copy(g, 3, me, left, to_across, gs_sem, gr_sem),
+            shard_copy(g, 4, to_near, left, to_across, gs_sem, gr_sem),
+            shard_copy(g, 5, to_across, right, to_near, gs_sem, gr_sem),
+        ]
+        shares = [
+            shard_copy(g, i, source, full, partner, rs_sem, rr_sem)
+            for i, source in enumerate((me, to_near, to_across, corner * 2 + core))
+        ]
+        return hops, shares
+
     for side in sides:
         side.wait()
     for g in range(groups):
@@ -298,8 +329,14 @@
             us[slots, cut] = second
             um[slots, cut] = fresh
             pr[slots, cut] = fresh.astype(jnp.bfloat16)
-        run(1, chips, lambda c: gather_copy(g, c).start())
-        own_relay(g).start()
+        if square:
+            hops, shares = square_copies(g)
+            for hop in hops[:4]:
+                hop.start()
+            shares[0].start()
+        else:
+            run(1, chips, lambda c: gather_copy(g, c).start())
+            own_relay(g).start()
     outs = [
         pltpu.make_async_copy(src, dst, side_sem.at[3 + i])
         for i, (src, dst) in enumerate(((um, um_hbm), (uf, uf_hbm), (us, us_hbm), (pr, gall.at[me])))
@@ -312,11 +349,37 @@
             gather_copy(g, c).wait_recv()
             relay_copy(g, c).start()
 
-        run(1, chips, relay)
+        if square:
+            hops, shares = square_copies(g)
+            hops[0].wait_recv()
+            hops[4].start()
+            hops[1].wait_recv()
+            hops[5].start()
+        else:
+            run(1, chips, relay)
+    if square:
+        for g in range(groups):
+            hops, shares = square_copies(g)
+            hops[2].wait_recv()
+            shares[1].start()
+            hops[3].wait_recv()
+            shares[2].start()
+        for g in range(groups):
+            hops, shares = square_copies(g)
+            hops[4].wait_recv()
+            hops[5].wait_recv()
+            shares[3].start()
     for g in range(groups):
-        own_relay(g).wait()
-        run(1, chips, lambda c: relay_copy(g, c).wait())
-        run(1, chips, lambda c: gather_copy(g, c).wait_send())
+        if square:
+            hops, shares = square_copies(g)
+            for share in shares:
+                share.wait()
+            for hop in hops:
+                hop.wait_send()
+        else:
+            own_relay(g).wait()
+            run(1, chips, lambda c: relay_copy(g, c).wait())
+            run(1, chips, lambda c: gather_copy(g, c).wait_send())
         run(0, CHUNKS, lambda q: run(1, n, lambda k: symbol_copy(g, q, k).wait_send()))
     run(1, n, lambda k: peak_copy(k).wait_send())
     for out in outs:
@@ -373,7 +436,7 @@
             dma((n,)),
             dma((groups, CHUNKS, n)),
             dma((groups, CHUNKS, n)),
-            *[dma((groups, n // 2))] * 4,
+            *[dma((groups, max(6, n // 2)))] * 4,
         ],
         compiler_params=pltpu.CompilerParams(
             collective_id=0, has_side_effects=True, vmem_limit_bytes=VMEM_LIMIT

time: 61.7 us -> 59.7 us (0.968)
  Pallas kernels: 60.8 us -> 58.8 us
    pallas_call x1, Pallas kernels: 54 us -> 52 us  [local(): pl.pallas_call(functools.partial(step_kernel, n), out_shape=(shard, shard...]
where the time goes in v3:
time: 59.7 us; the launch traced here: 59.4 us
  Pallas kernels  58.8 us (98%)
  between operations  0.64 us (1%)
    pallas_call x1, Pallas kernels, local(): pl.pallas_call(functools.partial(step_kernel, n), out_shape=(shard, shard...  52 us
    pallas_call x1, Pallas kernels, local(): pl.pallas_call(spread_kernel, grid=(8,), out_shape=(shard, shard, shard,...  6.77 us

profile of v3, /device:TPU:0, one launch (start us, length us, event | category | flops | bytes accessed | tf_op | source)
XLA Modules:
  0.0 59.4 jit_solution(1006860226568161468)
XLA Ops:
  0.6 52.0 %shard_map.111 = (f32[32,4096]{1,0:T(8,128)}, f32[32,4096]{1,0:T(8,128)}, f32[32,4096]{1,0:T(8,128)}, bf16[8,32,4096]{2,1,0:T(8,128)(2,1)}) custom-call(f32[256,4096]{1,0:T(8,128)} %bitcast.12, s32[256,4096]{1,0:T(8,128)} %bitcast.13, s32[1,4096]{1,0:T(1,128)} %bitcast.18, f32[16]{0:T(128)} %levels_ref.1, s32[1,256]{1,0:T(1,128)} %bitcast.19, ...), custom_call_target="tpu_custom_call" | custom-call | tf_op jit(solution)/shard_map/pallas_call | solution.py:411
  52.6 6.8 %shard_map.112 = (f32[32,4096]{1,0:T(8,128)}, f32[32,4096]{1,0:T(8,128)}, f32[32,4096]{1,0:T(8,128)}, bf16[256,4096]{1,0:T(8,128)(2,1)}) custom-call(s32[1,256]{1,0:T(1,128)} %bitcast.20, bf16[256,4096]{1,0:T(8,128)(2,1)} %bitcast.14, f32[32,4096]{1,0:T(8,128)} %get-tuple-element.13.um_in, f32[32,4096]{1,0:T(8,128)} %get-tuple-element.14.uf_in, ...), custom_call_target="tpu_custom_call" | custom-call | tf_op jit(solution)/shard_map/pallas_call | solution.py:451

commit v4 on v3

--- a/solution.py
+++ b/solution.py
@@ -400,7 +400,7 @@
     blocks, size = gradient.shape[2:]
     own = blocks // n
     tiles = size // TILE
-    row_chunks = 8
+    row_chunks = 4
     groups = slot_groups(own)
     f32, bf16 = jnp.float32, jnp.bfloat16
     hbm = pl.BlockSpec(memory_space=pl.ANY)
@@ -445,12 +445,12 @@
         gradient[0, 0], dither[0, 0], sign_bits.reshape(1, size), levels, layout_row,
         master[0], first_moment[0], second_moment[0],
     )
-    width = size // 8
+    width = size // 2
     wide = pl.BlockSpec((blocks, width), lambda i: (0, i))
     narrow = pl.BlockSpec((own, width), lambda i: (0, i))
     um, uf, us, parameters = pl.pallas_call(
         spread_kernel,
-        grid=(8,),
+        grid=(2,),
         out_shape=(shard, shard, shard, jax.ShapeDtypeStruct((blocks, size), bf16)),
         in_specs=[pl.BlockSpec((1, blocks), lambda i: (0, 0)), wide, narrow, narrow, narrow],
         out_specs=(narrow, narrow, narrow, wide),

time: 59.7 us -> 56.4 us (0.945)
  Pallas kernels: 58.8 us -> 55.5 us
    pallas_call x1, Pallas kernels: 6.77 us -> 3.87 us  [local(): pl.pallas_call(spread_kernel, grid=(2,), out_shape=(shard, shard, shard,...]
where the time goes in v4:
time: 56.4 us; the launch traced here: 56.2 us
  Pallas kernels  55.5 us (98%)
  between operations  0.64 us (1%)
    pallas_call x1, Pallas kernels, local(): pl.pallas_call(functools.partial(step_kernel, n), out_shape=(shard, shard...  51.7 us
    pallas_call x1, Pallas kernels, local(): pl.pallas_call(spread_kernel, grid=(2,), out_shape=(shard, shard, shard,...  3.87 us

profile of v4, /device:TPU:0, one launch (start us, length us, event | category | flops | bytes accessed | tf_op | source)
XLA Modules:
  0.0 56.2 jit_solution(10133941310265924849)
XLA Ops:
  0.6 51.7 %shard_map.111 = (f32[32,4096]{1,0:T(8,128)}, f32[32,4096]{1,0:T(8,128)}, f32[32,4096]{1,0:T(8,128)}, bf16[8,32,4096]{2,1,0:T(8,128)(2,1)}) custom-call(f32[256,4096]{1,0:T(8,128)} %bitcast.12, s32[256,4096]{1,0:T(8,128)} %bitcast.13, s32[1,4096]{1,0:T(1,128)} %bitcast.18, f32[16]{0:T(128)} %levels_ref.1, s32[1,256]{1,0:T(1,128)} %bitcast.19, ...), custom_call_target="tpu_custom_call" | custom-call | tf_op jit(solution)/shard_map/pallas_call | solution.py:411
  52.3 3.9 %shard_map.112 = (f32[32,4096]{1,0:T(8,128)}, f32[32,4096]{1,0:T(8,128)}, f32[32,4096]{1,0:T(8,128)}, bf16[256,4096]{1,0:T(8,128)(2,1)}) custom-call(s32[1,256]{1,0:T(1,128)} %bitcast.20, bf16[256,4096]{1,0:T(8,128)(2,1)} %bitcast.14, f32[32,4096]{1,0:T(8,128)} %get-tuple-element.13.um_in, f32[32,4096]{1,0:T(8,128)} %get-tuple-element.14.uf_in, ...), custom_call_target="tpu_custom_call" | custom-call | tf_op jit(solution)/shard_map/pallas_call | solution.py:451
